TPU v7x, 256 devices: a whole 4x4x8 slice. The times are simulated.
256 devices in a mesh: src: 32 (over y, z), tm: 8 (over x, core).
Axes of the slice: x: 4, y: 4, z: 8, core: 2. Of those that a mesh axis runs over, the one named last changes fastest.
Arguments:
- green: bfloat16 [8, 4096, 128, 128], P('tm', 'src'), may hold values from -0.046875 to 0.046875
- block_rows: int32 [8, 4096], P('tm', 'src'), may hold values from 0 to 31
- block_cols: int32 [8, 4096], P('tm', 'src'), may hold values from 0 to 31
- block_live: int32 [8, 4096], P('tm', 'src'), may hold values from 0 to 1, as said below
- data: float32 [8, 4096, 128], P('tm', 'src'), may hold values from -6 to 6
- row_weight: float32 [8, 4096], P('tm', 'src'), may hold values from 0.3 to 9
- source_gain: float32 [131072], P('src'), may hold values from 0.2 to 3
Outputs:
- solution: float32 [131072, 128], P(('src', 'tm'))
- residual: float32 [8, 4096, 128], P('tm', 'src')
- misfit: float32 [2, 128], replicated
Inputs may be any that keep to these rules, and one draw needn't show every extreme that they name: `block_live`: within one device's 128 slots every slot is live with the same chance, a chance that differs from device to device; in some device all 128 slots are live.
All inputs are finite; a program needn't handle non-finite values.
Results may differ from a plain program's by a relative error of at most 0.0038.
Values may be sent and summed in bfloat16 or wider, within the bound.
A program may use at most 128 MiB of HBM per device.

v0:
```python
import jax
import jax.numpy as jnp
from jax import lax
from jax.sharding import PartitionSpec as P

ITERS = 2


HIGH = lax.Precision.HIGHEST
EPSILON = 1e-06


def shards(green, block_rows, block_cols, block_live, data, row_weight, source_gain):
    blocks = green[0]
    slot_count = blocks.shape[0]
    block_size = blocks.shape[1]
    datasets = data.shape[2]
    own_rows = data.shape[1]
    own_blocks = own_rows // block_size
    groups = lax.axis_size("src")
    windows = lax.axis_size("tm")
    window_blocks = own_blocks * groups
    sources = source_gain.shape[0]
    col_blocks = sources // block_size
    share_rows = sources // windows
    total_rows = own_rows * groups * windows
    live_slots = block_live[0].astype(jnp.float32)[:, None]
    row_hit = block_rows[0][:, None] == jnp.arange(window_blocks, dtype=jnp.int32)[None, :]
    col_hit = block_cols[0][:, None] == jnp.arange(col_blocks, dtype=jnp.int32)[None, :]
    gather_rows = row_hit.astype(jnp.bfloat16)
    gather_cols = col_hit.astype(jnp.bfloat16)
    spread_rows = jnp.transpose(row_hit.astype(jnp.float32) * live_slots)
    spread_cols = jnp.transpose(col_hit.astype(jnp.float32) * live_slots)
    weight = row_weight[0][:, None]
    tm_index = lax.axis_index("tm")
    gain_group = source_gain[:, None]

    def adjoint(residual):
        sent = (weight * residual).astype(jnp.bfloat16).reshape(own_blocks, block_size * datasets)
        gathered = lax.all_gather(sent, "src", axis=0, tiled=True)
        picked = jnp.dot(gather_rows, gathered, preferred_element_type=jnp.bfloat16)
        products = jnp.einsum(
            "kac,kar->kcr",
            blocks,
            picked.reshape(slot_count, block_size, datasets),
            preferred_element_type=jnp.float32,
        )
        products = products.reshape(slot_count, block_size * datasets)
        return jnp.dot(spread_cols, products, precision=HIGH).reshape(sources, datasets)

    def steepest_of(residual):
        summed = lax.psum(adjoint(residual), "tm")
        steepest = gain_group * summed
        gamma_now = lax.psum(jnp.sum(steepest * steepest, axis=0), "src")
        return (steepest, gamma_now)

    residual = weight * data[0]
    steepest, gamma_now = steepest_of(residual)
    direction = steepest
    solution = jnp.zeros((share_rows, datasets), jnp.float32)
    misfits = []
    for iteration in range(ITERS):
        forward_picked = jnp.dot(
            gather_cols,
            (gain_group * direction)
            .astype(jnp.bfloat16)
            .reshape(col_blocks, block_size * datasets),
            preferred_element_type=jnp.bfloat16,
        )
        forward_products = jnp.einsum(
            "kac,kcr->kar",
            blocks,
            forward_picked.reshape(slot_count, block_size, datasets),
            preferred_element_type=jnp.float32,
        )
        forward_products = forward_products.reshape(slot_count, block_size * datasets)
        forward_summed = lax.psum_scatter(
            jnp.dot(spread_rows, forward_products, precision=HIGH),
            "src",
            scatter_dimension=0,
            tiled=True,
        )
        image = weight * forward_summed.reshape(own_rows, datasets)
        image_norm = lax.psum(jnp.sum(image * image, axis=0), ("src", "tm"))
        step_size = gamma_now / (image_norm + EPSILON)
        solution = solution + step_size * lax.dynamic_slice_in_dim(
            direction, tm_index * share_rows, share_rows, 0
        )
        residual = residual - step_size * image
        misfits.append(lax.psum(jnp.sum(residual * residual, axis=0), ("src", "tm")) / total_rows)
        if iteration + 1 < ITERS:
            steepest, gamma_next = steepest_of(residual)
            direction = steepest + gamma_next / (gamma_now + EPSILON) * direction
            gamma_now = gamma_next
    return (solution, residual[None], jnp.stack(misfits))


def solution(mesh):
    placed = (
        P("tm", "src", None, None),
        P("tm", "src"),
        P("tm", "src"),
        P("tm", "src"),
        P("tm", "src", None),
        P("tm", "src"),
        P("src"),
    )
    return jax.shard_map(
        shards,
        mesh=mesh,
        in_specs=placed,
        out_specs=(P(("src", "tm"), None), P("tm", "src", None), P()),
        check_vma=False,
    )
```

profile of v0, /device:TPU:1, one launch (start us, length us, event | category | flops | bytes accessed | tf_op | source)
XLA Modules:
  0.0 1052.1 jit_solution(14238654614562010378)
XLA Ops:
  7.2 0.7 mul.232
  7.9 1.6 convert_bitcast_fusion.1
  9.6 0.7 convert_bitcast_fusion.2
  10.2 78.8 %all-gather.5.cloned.1.call-done = bf16[32,1,16384]{2,1,0:T(2,128)(2,1)} async-done(((bf16[1,1,16384]{2,1,0:T(2,128)(2,1)}), bf16[32,1,16384]{2,1,0:T(2,128)(2,1)}) %all-gather.5.cloned.1.call-update) | async-done | bytes 1048592 | tf_op jit(solution)/shard_map/all_gather | solution.py:40
  89.1 3.2 convolution_bitcast_fusion.1
  92.3 1.2 copy.42
  93.5 0.9 copy-done
  94.5 4.8 fusion.10
  99.2 9.3 copy.27
  108.6 10.7 %fusion.43 = f32[32,16384]{1,0:T(8,128)S(1)} fusion(f32[128,16384]{0,1:T(8,128)} %bitcast.97, f32[128]{0:T(128)S(1)} %convert_bitcast_fusion.2, s32[128]{0:T(128)S(1)} %bitcast.117), kind=kOutput, calls=%fused_computation.48 | convolution fusion | flops 805314560 | bytes 10486784 | tf_op jit(solution)/shard_map/dot_general | solution.py:49
  119.3 1.5 reshape.248
  121.3 69.5 %all-reduce.8.cloned.1.call-done = f32[4096,128]{1,0:T(8,128)} async-done(((f32[4096,128]{1,0:T(8,128)}), f32[4096,128]{1,0:T(8,128)}) %all-reduce.8.cloned.1.call-update) | async-done | bytes 2097168 | tf_op jit(solution)/shard_map/psum | solution.py:52
  190.9 1.9 multiply_convert_fusion.1
  192.8 1.3 reshape.249
  194.1 2.7 fusion.29
  196.8 7.3 fusion.13
  204.1 9.4 copy.30
  213.4 11.7 %fusion.39 = f32[32,16384]{1,0:T(8,128)} fusion(f32[128,16384]{0,1:T(8,128)} %bitcast.98, s32[128]{0:T(128)S(1)} %bitcast.122, f32[128]{0:T(128)S(1)} %convert_bitcast_fusion.2), kind=kOutput, calls=%fused_computation.44 | convolution fusion | flops 805314560 | bytes 10486784 | tf_op jit(solution)/shard_map/dot_general | solution.py:78
  225.2 0.6 dynamic-slice
  226.4 61.0 %psum.57 = f32[128]{0:T(128)S(1)} all-reduce(f32[128]{0:T(128)S(1)} %multiply_reduce_fusion.1), channel_id=1, replica_groups=mesh['src'=32,'tm'=8] {'src'}, use_global_device_ids=true, to_apply=%region_2.0 | all-reduce | flops 128 | bytes 1024 | tf_op jit(solution)/shard_map/psum | solution.py:54
  287.4 89.4 %all-reduce.12.cloned.1.call-done = f32[32,16384]{1,0:T(8,128)} async-done(((f32[32,16384]{1,0:T(8,128)}), f32[32,16384]{1,0:T(8,128)}) %all-reduce.12.cloned.1.call-update) | async-done | bytes 2097168
  376.8 1.7 constant_dynamic-slice_fusion.1
  378.6 78.4 %psum.58 = f32[128]{0:T(128)S(1)} all-reduce(f32[128]{0:T(128)S(1)} %multiply_reduce_fusion.5), channel_id=1, replica_groups=mesh['src'=32,'tm'=8] {'src','tm'}, use_global_device_ids=true, to_apply=%region_5.0 | all-reduce | flops 128 | bytes 1024 | tf_op jit(solution)/shard_map/psum | solution.py:84
  457.0 2.4 convert_bitcast_fusion
  459.7 69.4 %all-gather.7.cloned.1.call-done = bf16[32,1,16384]{2,1,0:T(2,128)(2,1)} async-done(((bf16[1,1,16384]{2,1,0:T(2,128)(2,1)}), bf16[32,1,16384]{2,1,0:T(2,128)(2,1)}) %all-gather.7.cloned.1.call-update) | async-done | bytes 1048592 | tf_op jit(solution)/shard_map/all_gather | solution.py:40
  529.1 3.2 convolution_bitcast_fusion
  532.3 1.2 copy.43
  533.6 0.9 copy-done.2
  534.5 4.7 fusion.18
  539.2 9.4 copy.32
  548.6 11.7 %fusion.41 = f32[32,16384]{1,0:T(8,128)} fusion(f32[128,16384]{0,1:T(8,128)} %bitcast.99, f32[128]{0:T(128)S(1)} %convert_bitcast_fusion.2, s32[128]{0:T(128)S(1)} %bitcast.119), kind=kOutput, calls=%fused_computation.46 | convolution fusion | flops 805314560 | bytes 10486784 | tf_op jit(solution)/shard_map/dot_general | solution.py:49
  560.3 2.7 reshape.254
  563.0 70.0 %all-reduce.10.cloned.1.call-done = f32[4096,128]{1,0:T(8,128)} async-done(((f32[4096,128]{1,0:T(8,128)}), f32[4096,128]{1,0:T(8,128)}) %all-reduce.10.cloned.1.call-update) | async-done | bytes 2097168 | tf_op jit(solution)/shard_map/psum | solution.py:52
  633.1 1.9 multiply_reduce_fusion
  635.0 61.2 %psum.60 = f32[128]{0:T(128)S(1)} all-reduce(f32[128]{0:T(128)S(1)} %multiply_reduce_fusion), channel_id=1, replica_groups=mesh['src'=32,'tm'=8] {'src'}, use_global_device_ids=true, to_apply=%region_8.0 | all-reduce | flops 128 | bytes 1024 | tf_op jit(solution)/shard_map/psum | solution.py:54
  696.2 3.3 multiply_convert_fusion
  699.4 1.5 reshape.255
  701.0 1.3 fusion.26
  702.3 0.9 copy-done.3
  703.2 7.3 fusion.21
  710.4 9.4 copy.35
  719.8 11.7 %fusion.37 = f32[32,16384]{1,0:T(8,128)} fusion(f32[128,16384]{0,1:T(8,128)} %bitcast.96, s32[128]{0:T(128)S(1)} %bitcast.124, f32[128]{0:T(128)S(1)} %convert_bitcast_fusion.2), kind=kOutput, calls=%fused_computation.42 | convolution fusion | flops 805314560 | bytes 10486784 | tf_op jit(solution)/shard_map/dot_general | solution.py:78
  731.6 157.0 %all-reduce.14.cloned.1.call-done = f32[32,16384]{1,0:T(8,128)} async-done(((f32[32,16384]{1,0:T(8,128)}), f32[32,16384]{1,0:T(8,128)}) %all-reduce.14.cloned.1.call-update) | async-done | bytes 2097168
  888.6 1.7 constant_dynamic-slice_fusion
  890.4 78.4 %psum.61 = f32[128]{0:T(128)S(1)} all-reduce(f32[128]{0:T(128)S(1)} %multiply_reduce_fusion.4), channel_id=1, replica_groups=mesh['src'=32,'tm'=8] {'src','tm'}, use_global_device_ids=true, to_apply=%region_11.0 | all-reduce | flops 128 | bytes 1024 | tf_op jit(solution)/shard_map/psum | solution.py:84
  968.9 73.1 %all-reduce.2 = (f32[128]{0:T(128)S(1)}, f32[128]{0:T(128)S(1)}) all-reduce(f32[128]{0:T(128)S(1)} %get-tuple-element.4, f32[128]{0:T(128)S(1)} %get-tuple-element.3), channel_id=1, replica_groups=mesh['src'=32,'tm'=8] {'src','tm'}, use_global_device_ids=true, to_apply=%region_15.0 | all-reduce | flops 256 | bytes 2048 | tf_op jit(solution)/shard_map/psum | solution.py:90
  1042.6 0.7 multiply_subtract_fusion
  1043.3 1.7 multiply_add_fusion.1
  (39 shorter events, 2.5 us)
Async XLA Ops:
  7.2 81.9 %all-gather.5.cloned.1.call-start = ((), (), s32[]{:S(2)}) async-start(), calls=%async_computation.2 | async-start | bytes 2162688 | tf_op jit(solution)/shard_map/all_gather | solution.py:40
  9.5 181.3 %all-reduce.8.cloned.1.call-start = ((), (), s32[]{:S(2)}) async-start(), calls=%async_computation | async-start | bytes 4194304 | tf_op jit(solution)/shard_map/psum | solution.py:52
  92.3 2.2 copy-start
  99.2 9.3 copy-start.7
  119.3 71.6 %copy-start.5 = (f32[4096]{0:T(1024)S(1)}, f32[4096]{0:T(1024)}, u32[]{:S(2)}) copy-start(f32[4096]{0:T(1024)} %param.13) | copy-start | bytes 49156
  120.8 256.0 %all-reduce.12.cloned.1.call-start = ((), (), s32[]{:S(2)}) async-start(), calls=%async_computation.4 | async-start | bytes 4194304
  194.1 2.7 copy-start.1
  204.1 9.4 copy-start.8
  213.4 11.8 %copy-start.9 = (u32[256]{0:T(256)S(1)}, u32[256]{0:T(256)}, u32[]{:S(2)}) copy-start(u32[256]{0:T(256)} %constant.28) | copy-start | bytes 3076
  225.1 153.4 %copy-start.6 = (f32[1,128]{1,0:T(1,128)S(1)}, f32[1,128]{1,0:T(1,128)}, u32[]{:S(2)}) copy-start(f32[1,128]{1,0:T(1,128)} %param.12) | copy-start | bytes 1540
  225.2 303.9 %all-gather.7.cloned.1.call-start = ((), (), s32[]{:S(2)}) async-start(), calls=%async_computation.3 | async-start | bytes 2162688 | tf_op jit(solution)/shard_map/all_gather | solution.py:40
  459.5 173.6 %all-reduce.10.cloned.1.call-start = ((), (), s32[]{:S(2)}) async-start(), calls=%async_computation.1 | async-start | bytes 4194304 | tf_op jit(solution)/shard_map/psum | solution.py:52
  532.3 2.2 copy-start.2
  563.0 325.6 %all-reduce.14.cloned.1.call-start = ((), (), s32[]{:S(2)}) async-start(), calls=%async_computation.5 | async-start | bytes 4194304
  701.0 2.2 copy-start.3
  719.8 249.0 %copy-start.4 = (f32[1,128,128]{2,1,0:T(8,128)S(1)}, f32[1,128,128]{2,1,0:T(8,128)}, u32[]{:S(2)}) copy-start(f32[1,128,128]{2,1,0:T(8,128)} %param.11) | copy-start | bytes 196612
Sparse Core Ops, SparseCore 0:
  11.2 77.8 all-gather.4
  120.9 69.8 all-reduce.7
  225.3 151.4 all-reduce.11
  459.6 69.4 all-gather.6
  563.1 69.8 all-reduce.9
  731.7 156.8 all-reduce.13
where the time goes:
time: 1060 us; the launch traced here: 1050 us
  waiting for transfers between devices  534 us (50%)
  blocking collectives  352 us (33%)
  matrix products  80.3 us (8%)
  local copies, waits for them, and re-layouts  54.4 us (5%)
  other arithmetic  15.6 us (1%)
  between operations  14.5 us (1%)
    unnamed x8, waiting for transfers between devices  247 us
    psum x2, blocking collectives, shards(): image_norm = lax.psum(jnp.sum(image * image, axis=0), ('src', 'tm'))  157 us
    all_gather x2, waiting for transfers between devices, adjoint(): gathered = lax.all_gather(sent, 'src', axis=0, tiled=True)  148 us
    psum x2, waiting for transfers between devices, steepest_of(): summed = lax.psum(adjoint(residual), 'tm')  140 us
    psum x2, blocking collectives, steepest_of(): gamma_now = lax.psum(jnp.sum(steepest * steepest, axis=0), 'src')  122 us
    psum x1, blocking collectives, shards(): lax.psum(jnp.sum(residual * residual, axis=0), ('src', 'tm')) / total_rows  73.1 us
    dot_general x2, matrix products, shards(): jnp.dot(spread_rows, forward_products, precision=HIGH)  23.4 us
    dot_general x2, matrix products, adjoint(): jnp.dot(spread_cols, products, precision=HIGH).reshape(sources, datasets)  22.4 us
  transfers between devices with their start and end apart: 6, of which 6 were waited for; matrix products, arithmetic and copies ran while one was open for 0% of the time, Pallas kernels for 0%

commit v1 on v0

v1 whole, which is shorter than its diff:
```python
import functools

import jax
import jax.numpy as jnp
from jax import lax
from jax.experimental import pallas as pl
from jax.experimental.pallas import tpu as pltpu
from jax.sharding import PartitionSpec as P

MESH = pl.DeviceIdType.MESH
EPSILON = 1e-06
NZ = 8
NC = 2
BS = 128
F32 = jnp.float32
BF16 = jnp.bfloat16


STEPS = 32000.0


def outward(n):
    return sorted(range(1, n), key=lambda d: -min(d, n - d))


def pack(ref, v):
    top = jnp.maximum(jnp.max(jnp.abs(v), axis=0, keepdims=True), 1e-30)
    e = jnp.ceil(jnp.log2(top))
    q = jnp.floor(v * (jnp.exp2(-e) * STEPS) + 0.5)
    ref[0:BS, :] = q.astype(jnp.int32).astype(jnp.int16)
    ref[BS : BS + 16, :] = jnp.broadcast_to(e.astype(jnp.int32), (16, BS)).astype(jnp.int16)


def unpack(ref):
    e = ref[BS : BS + 16, :].astype(jnp.int32).astype(F32)[0:1]
    return ref[0:BS, :].astype(jnp.int32).astype(F32) * (jnp.exp2(e) * (1.0 / STEPS))


def kernel(
    ny, nx, total_rows, slots, cb,
    tab, green_hbm, data, weight, gain,
    sol_out, res_out, mis_out,
    green, ag, sums, core_send, core_recv, x_send, x_recv, tb, y_send, y_recv, z_send, z_recv,
    wcol, gcol, steep, own, ar_z, ar_p, ar_c,
    ssem, rsem, lsem,
):
    nz, nc = NZ, NC
    rb = ny * nz
    per = cb // (nx * nc)
    s = lax.axis_index("src")
    t = lax.axis_index("tm")
    y, z = s // nz, s % nz
    x, c = t // nc, t % nc

    def zdev(d):
        return (y * nz + (z + d) % nz, t)

    def ydev(d):
        return (((y + d) % ny) * nz + z, t)

    def xdev(d):
        return (s, ((x + d) % nx) * nc + c)

    def cdev():
        return (s, x * nc + (1 - c))

    counter = [0]

    def rcopy(src, dst, dev):
        i = counter[0]
        counter[0] += 1
        return pltpu.make_async_remote_copy(
            src_ref=src, dst_ref=dst, send_sem=ssem.at[i], recv_sem=rsem.at[i],
            device_id=dev, device_id_type=MESH,
        )

    load = pltpu.make_async_copy(green_hbm, green, lsem)
    load.start()

    def pdev(d):
        return (((y + d // nx) % ny) * nz + z, ((x + d % nx) % nx) * nc + c)

    peers = [zdev(d) for d in range(1, nz)] + [pdev(d) for d in range(1, ny * nx)] + [cdev()]
    barrier = pltpu.get_barrier_semaphore()
    for dev in peers:
        pl.semaphore_signal(barrier, inc=1, device_id=dev, device_id_type=MESH)

    wcol[...] = jnp.transpose(jnp.broadcast_to(weight[...], (BS, BS)))
    for i in range(per):
        row = gain[pl.ds(t * per + i, 1), :]
        gcol[i] = jnp.transpose(jnp.broadcast_to(row, (BS, BS)))
    sums[slots] = jnp.zeros((BS, BS), F32)
    res_out[...] = wcol[...] * data[...]
    pl.semaphore_wait(barrier, len(peers))

    def gather_src(it):
        ag[it, y, z] = jnp.transpose(wcol[...] * res_out[...]).astype(BF16)
        mine = ag.at[it, y, z]
        zc = {d: rcopy(mine, mine, zdev(d)) for d in outward(nz)}
        yc = [rcopy(mine, mine, ydev(e)) for e in outward(ny)]
        for d in outward(nz):
            zc[d].start()
        for cp in yc:
            cp.start()
        for d in reversed(outward(nz)):
            zc[d].wait_recv()
            got = ag.at[it, y, (z + nz - d) % nz]
            for e in outward(ny):
                cp = rcopy(got, got, ydev(e))
                cp.start()
                yc.append(cp)
        for cp in yc:
            cp.wait()
        for d in zc:
            zc[d].wait_send()

    def adjoint(it):
        def slot(k, carry):
            r = tab[0, k]
            p = jnp.dot(ag[it, r // nz, r % nz], green[k], preferred_element_type=F32)
            sums[k] = p + sums[tab[2, k]]
            return carry

        lax.fori_loop(0, slots, slot, 0, unroll=4)

    def forward(it):
        def slot(k, carry):
            p = jnp.dot(green[k], tb[it, tab[1, k]], preferred_element_type=F32)
            sums[k] = p + sums[tab[3, k]]
            return carry

        lax.fori_loop(0, slots, slot, 0, unroll=4)

    def scatter_tm(it):
        order = outward(nx) + [0]
        cc = []
        for d in order:
            xx = (x + d) % nx
            for i in range(per):
                b = xx * nc * per + (1 - c) * per + i
                core_send[it, xx * per + i] = sums[tab[4, b]]
            part = pl.ds(xx * per, per)
            cp = rcopy(core_send.at[it, part], core_recv.at[it, part], cdev())
            cp.start()
            cc.append(cp)
        xc = []
        for j, d in enumerate(order):
            xx = (x + d) % nx
            cc[j].wait()
            for i in range(per):
                b = xx * nc * per + c * per + i
                v = sums[tab[4, b]] + core_recv[it, xx * per + i]
                if d:
                    pack(x_send.at[it, d - 1, i], v)
                else:
                    own[i] = v
            if d:
                cp = rcopy(x_send.at[it, d - 1], x_recv.at[it, d - 1], xdev(d))
                cp.start()
                xc.append(cp)
        for cp in xc:
            cp.wait()
        gamma = jnp.zeros((1, BS), F32)
        for i in range(per):
            v = own[i]
            for d in range(1, nx):
                v = v + unpack(x_recv.at[it, d - 1, i])
            st = gcol[i] * jnp.transpose(v)
            steep[it, i] = st
            gamma = gamma + jnp.sum(st * st, axis=0, keepdims=True)
            tb[it, t * per + i] = (gcol[i] * st).astype(BF16)
        return gamma

    def gather_tm(it):
        def part(xx, cc):
            return tb.at[it, pl.ds((xx * nc + cc) * per, per)]

        mine = part(x, c)
        xc = {d: rcopy(mine, mine, xdev(d)) for d in outward(nx)}
        for d in xc:
            xc[d].start()
        fc = [rcopy(mine, mine, cdev())]
        fc[0].start()
        for d in reversed(outward(nx)):
            xc[d].wait_recv()
            got = part((x + nx - d) % nx, c)
            cp = rcopy(got, got, cdev())
            cp.start()
            fc.append(cp)
        for cp in fc:
            cp.wait()
        for d in xc:
            xc[d].wait_send()

    def scatter_src(it):
        order = outward(nz) + [0]
        yc = {}
        for d in order:
            zz = (z + d) % nz
            for e in outward(ny):
                pack(y_send.at[it, e - 1, zz], sums[tab[5, ((y + e) % ny) * nz + zz]])
                yc[d, e] = rcopy(y_send.at[it, e - 1, zz], y_recv.at[it, e - 1, zz], ydev(e))
                yc[d, e].start()
        zc = []
        for d in order:
            zz = (z + d) % nz
            v = sums[tab[5, y * nz + zz]]
            for e in range(1, ny):
                yc[d, e].wait()
                v = v + unpack(y_recv.at[it, e - 1, zz])
            if d:
                pack(z_send.at[it, d - 1], v)
                cp = rcopy(z_send.at[it, d - 1], z_recv.at[it, d - 1], zdev(d))
                cp.start()
                zc.append(cp)
        for cp in zc:
            cp.wait()
        for d in range(1, nz):
            v = v + unpack(z_recv.at[it, d - 1])
        return wcol[...] * v

    def all_reduce(n, v):
        for ref, me, count, dev in (
            (ar_z, z, nz, zdev), (ar_p, y * nx + x, ny * nx, pdev), (ar_c, c, nc, None),
        ):
            ref[n, me] = v
            copies = [
                rcopy(ref.at[n, me], ref.at[n, me], dev(d) if dev else cdev())
                for d in range(count - 1, 0, -1)
            ]
            for cp in copies:
                cp.start()
            for cp in copies:
                cp.wait()
            v = ref[n, 0]
            for j in range(1, count):
                v = v + ref[n, j]
        return v

    def rowsum(a):
        return jnp.sum(a, axis=0, keepdims=True)

    gather_src(0)
    load.wait()
    adjoint(0)
    gamma0 = scatter_tm(0)
    gather_tm(0)
    forward(0)
    image0 = scatter_src(0)
    norms = jnp.concatenate([gamma0, rowsum(image0 * image0), jnp.zeros((6, BS), F32)], axis=0)
    norms = all_reduce(0, norms)
    gamma0 = norms[0:1]
    norm0 = norms[1:2]
    alpha0 = gamma0 / (norm0 + EPSILON)
    own[per] = image0
    residual = res_out[...] - alpha0 * image0
    res_out[...] = residual
    gather_src(1)
    adjoint(1)
    gamma1 = scatter_tm(1)
    gather_tm(1)
    forward(1)
    part1 = scatter_src(1)
    image0 = own[per]
    residual = res_out[...]
    norms = jnp.concatenate(
        [
            gamma1, rowsum(part1 * part1), rowsum(part1 * image0), rowsum(residual * residual),
            rowsum(residual * part1), rowsum(residual * image0), jnp.zeros((2, BS), F32),
        ],
        axis=0,
    )
    norms = all_reduce(1, norms)
    gamma1 = norms[0:1]
    beta = gamma1 / (gamma0 + EPSILON)
    norm1 = norms[1:2] + beta * (2.0 * norms[2:3] + beta * norm0)
    alpha1 = gamma1 / (norm1 + EPSILON)
    cross = norms[4:5] + beta * norms[5:6]
    misfit1 = norms[3:4] + alpha1 * (alpha1 * norm1 - 2.0 * cross)
    mis_out[0:1, :] = norms[3:4] / total_rows
    mis_out[1:2, :] = misfit1 / total_rows
    res_out[...] = residual - alpha1 * (part1 + beta * image0)
    for i in range(per):
        sol_out[pl.ds(i * BS, BS), :] = (alpha0 + alpha1 * beta) * steep[0, i] + alpha1 * steep[1, i]


def tables(rows, cols, live, slots, rb, cb):
    j = jnp.arange(slots, dtype=jnp.int32)
    lived = live != 0
    before = (j[None, :] < j[:, None]) & lived[None, :]

    def prev(key):
        return jnp.max(jnp.where(before & (key[None, :] == key[:, None]), j[None, :], -1), axis=1)

    def last(key):
        hit = lived[None, :] & (key[None, :] == j[:, None])
        return jnp.max(jnp.where(hit, j[None, :], -1), axis=1)

    out = jnp.stack([rows, cols, prev(cols), prev(rows), last(cols), last(rows), rows, cols])
    return jnp.where(out < 0, slots, out)


def shards(green, block_rows, block_cols, block_live, data, row_weight, source_gain):
    slots = green.shape[1]
    src, tm = lax.axis_size("src"), lax.axis_size("tm")
    ny, nx = src // NZ, tm // NC
    cb = source_gain.shape[0] // BS
    rb = src
    per = cb // tm
    datasets = data.shape[2]
    tab = tables(block_rows[0], block_cols[0], block_live[0], slots, rb, cb)
    src_copies = (NZ - 1) + (ny - 1) * NZ
    tm_copies = nx + (nx - 1) + (nx - 1) + nx
    copies = 2 * (2 * src_copies + tm_copies + (NZ - 1) + (ny * nx - 1) + (NC - 1))
    vmem = pl.BlockSpec(memory_space=pltpu.VMEM)
    tile = (BS, BS)
    coded = (BS + 16, BS)
    sol, res, mis = pl.pallas_call(
        functools.partial(kernel, ny, nx, float(src * tm * BS), slots, cb),
        out_shape=(
            jax.ShapeDtypeStruct((per * BS, datasets), F32),
            jax.ShapeDtypeStruct(tile, F32),
            jax.ShapeDtypeStruct((2, datasets), F32),
        ),
        in_specs=[
            pl.BlockSpec(memory_space=pltpu.SMEM),
            pl.BlockSpec(memory_space=pl.ANY),
            vmem, vmem, vmem,
        ],
        out_specs=(vmem, vmem, vmem),
        scratch_shapes=[
            pltpu.VMEM((slots,) + tile, BF16),
            pltpu.VMEM((2, ny, NZ) + tile, BF16),
            pltpu.VMEM((slots + 1,) + tile, F32),
            pltpu.VMEM((2, nx * per) + tile, F32),
            pltpu.VMEM((2, nx * per) + tile, F32),
            pltpu.VMEM((2, nx - 1, per) + coded, jnp.int16),
            pltpu.VMEM((2, nx - 1, per) + coded, jnp.int16),
            pltpu.VMEM((2, cb) + tile, BF16),
            pltpu.VMEM((2, ny - 1, NZ) + coded, jnp.int16),
            pltpu.VMEM((2, ny - 1, NZ) + coded, jnp.int16),
            pltpu.VMEM((2, NZ - 1) + coded, jnp.int16),
            pltpu.VMEM((2, NZ - 1) + coded, jnp.int16),
            pltpu.VMEM(tile, F32),
            pltpu.VMEM((per,) + tile, F32),
            pltpu.VMEM((2, per) + tile, F32),
            pltpu.VMEM((per + 1,) + tile, F32),
            pltpu.VMEM((2, NZ, 8, BS), F32),
            pltpu.VMEM((2, ny * nx, 8, BS), F32),
            pltpu.VMEM((2, NC, 8, BS), F32),
            pltpu.SemaphoreType.DMA((copies,)),
            pltpu.SemaphoreType.DMA((copies,)),
            pltpu.SemaphoreType.DMA,
        ],
        compiler_params=pltpu.CompilerParams(
            collective_id=0, has_side_effects=True, vmem_limit_bytes=48 * 1024 * 1024
        ),
    )(tab, green[0], data[0], row_weight, source_gain.reshape(cb, BS))
    return sol, res[None], mis


def solution(mesh):
    placed = (
        P("tm", "src", None, None),
        P("tm", "src"),
        P("tm", "src"),
        P("tm", "src"),
        P("tm", "src", None),
        P("tm", "src"),
        P("src"),
    )
    return jax.shard_map(
        shards,
        mesh=mesh,
        in_specs=placed,
        out_specs=(P(("src", "tm"), None), P("tm", "src", None), P()),
        check_vma=False,
    )
```

time: 1060 us -> 184 us (0.17)
  waiting for transfers between devices: 534 us -> 0 us
  blocking collectives: 352 us -> 0 us
  Pallas kernels: 0 us -> 174 us
  matrix products: 80.3 us -> 0 us
  local copies, waits for them, and re-layouts: 54.4 us -> 7.05 us
  other arithmetic: 15.6 us -> 1.61 us
  between operations: 14.5 us -> 0.66 us
    psum x5 -> x0, blocking collectives: 352 us -> none  [the longest x2 157 us: shards(): image_norm = lax.psum(jnp.sum(image * image, axis=0), ('src', 'tm'))]
    unnamed x8 -> x0, waiting for transfers between devices: 247 us -> none
    pallas_call x0 -> x1, Pallas kernels: none -> 174 us  [shards(): pl.pallas_call(functools.partial(kernel, ny, nx, float(src * tm * BS), sl...]
    all_gather x2 -> x0, waiting for transfers between devices: 148 us -> none  [adjoint(): gathered = lax.all_gather(sent, 'src', axis=0, tiled=True)]
    psum x2 -> x0, waiting for transfers between devices: 140 us -> none  [steepest_of(): summed = lax.psum(adjoint(residual), 'tm')]
    dot_general x12 -> x0, matrix products: 80.3 us -> none  [the longest x2 23.4 us: shards(): jnp.dot(spread_rows, forward_products, precision=HIGH)]
    dot_general x4 -> x0, local copies, waits for them, and re-layouts: 37.4 us -> none  [the longest x2 18.7 us: shards(): jnp.einsum('kac,kcr->kar', blocks, forward_picked.reshape(slot_count, blo...]
  transfers between devices with their start and end apart: 6 -> 0, of which waited for: 6 -> 0; matrix products, arithmetic and copies ran while one was open for 0% -> 0% of each run, Pallas kernels for 0% -> 0%
where the time goes in v1:
time: 184 us
  Pallas kernels  174 us (95%)
  local copies, waits for them, and re-layouts  7.05 us (4%)
    pallas_call x1, Pallas kernels, shards(): pl.pallas_call(functools.partial(kernel, ny, nx, float(src * tm * BS), sl...  174 us
    unnamed x11, local copies, waits for them, and re-layouts  6.29 us

profile of v1, /device:TPU:1, one launch (start us, length us, event | category | flops | bytes accessed | tf_op | source)
XLA Modules:
  0.0 183.7 jit_solution(1149479943477342373)
XLA Ops:
  0.6 0.7 compare_bitcast_fusion
  1.3 0.9 select_reduce_fusion
  2.2 0.8 stack.19
  3.0 0.0 copy-start
  3.0 2.2 %copy-done = bf16[1,128,128,128]{3,2,1,0:T(8,128)(2,1)S(1)} copy-done((bf16[1,128,128,128]{3,2,1,0:T(8,128)(2,1)S(1)}, bf16[1,128,128,128]{3,2,1,0:T(8,128)(2,1)}, u32[]{:S(2)}) %copy-start) | copy-done | bytes 4194328
  5.2 0.0 copy-start.1
  5.2 0.8 copy-done.1
  6.0 0.0 copy-start.2
  6.0 0.7 copy-done.2
  6.8 0.0 copy-start.3
  6.8 0.7 copy-done.3
  7.4 174.3 %shard_map.94 = (f32[512,128]{1,0:T(8,128)S(1)}, f32[128,128]{1,0:T(8,128)S(1)}, f32[2,128]{1,0:T(2,128)S(1)}) custom-call(s32[8,128]{1,0:T(8,128)S(1)} %compare_select_fusion.tab, bf16[128,128,128]{2,1,0:T(8,128)(2,1)S(1)} %bitcast.12, f32[128,128]{1,0:T(8,128)S(1)} %bitcast.14, f32[1,128]{1,0:T(1,128)S(1)} %copy-done.3, f32[32,128]{1,0:T(8,128)S(1)} %bitcast.15), custom_call_target="tpu_custom_call" | custom-call | tf_op jit(solution)/shard_map/pallas_call | solution.py:318
  181.8 0.7 copy.13
  182.5 0.6 copy.14
  183.1 0.6 copy.15
  (1 shorter events, 0.0 us)
Async XLA Ops:
  3.0 2.2 %copy-start = (bf16[1,128,128,128]{3,2,1,0:T(8,128)(2,1)S(1)}, bf16[1,128,128,128]{3,2,1,0:T(8,128)(2,1)}, u32[]{:S(2)}) copy-start(bf16[1,128,128,128]{3,2,1,0:T(8,128)(2,1)} %param.7) | copy-start | bytes 12582916
  5.2 0.8 copy-start.1
  6.0 0.7 copy-start.2
  6.8 0.7 copy-start.3

commit v2 on v1

--- a/solution.py
+++ b/solution.py
@@ -38,9 +38,9 @@
 
 def kernel(
     ny, nx, total_rows, slots, cb,
-    tab, green_hbm, data, weight, gain,
+    tab, green_hbm, data_hbm, weight_hbm, gain_hbm,
     sol_out, res_out, mis_out,
-    green, ag, sums, core_send, core_recv, x_send, x_recv, tb, y_send, y_recv, z_send, z_recv,
+    green, data, weight, gain, ag, wire, acol, sums, core_send, core_recv, x_send, x_recv, tb, y_send, y_recv, z_send, z_recv,
     wcol, gcol, steep, own, ar_z, ar_p, ar_c,
     ssem, rsem, lsem,
 ):
@@ -74,8 +74,10 @@
             device_id=dev, device_id_type=MESH,
         )
 
-    load = pltpu.make_async_copy(green_hbm, green, lsem)
-    load.start()
+    pairs = ((weight_hbm, weight), (data_hbm, data), (gain_hbm, gain), (green_hbm, green))
+    loads = [pltpu.make_async_copy(a, b, lsem.at[i]) for i, (a, b) in enumerate(pairs)]
+    for cp in loads:
+        cp.start()
 
     def pdev(d):
         return (((y + d // nx) % ny) * nz + z, ((x + d % nx) % nx) * nc + c)
@@ -85,6 +87,8 @@
     for dev in peers:
         pl.semaphore_signal(barrier, inc=1, device_id=dev, device_id_type=MESH)
 
+    for cp in loads[:3]:
+        cp.wait()
     wcol[...] = jnp.transpose(jnp.broadcast_to(weight[...], (BS, BS)))
     for i in range(per):
         row = gain[pl.ds(t * per + i, 1), :]
@@ -93,35 +97,52 @@
     res_out[...] = wcol[...] * data[...]
     pl.semaphore_wait(barrier, len(peers))
 
-    def gather_src(it):
-        ag[it, y, z] = jnp.transpose(wcol[...] * res_out[...]).astype(BF16)
-        mine = ag.at[it, y, z]
+    def gather_begin(it, v):
+        pack(wire.at[it, y, z], jnp.transpose(v))
+        mine = wire.at[it, y, z]
         zc = {d: rcopy(mine, mine, zdev(d)) for d in outward(nz)}
-        yc = [rcopy(mine, mine, ydev(e)) for e in outward(ny)]
+        yc = [(rcopy(mine, mine, ydev(e)), e, z) for e in outward(ny)]
         for d in outward(nz):
             zc[d].start()
-        for cp in yc:
+        for cp, e, zz in yc:
             cp.start()
+        return zc, yc
+
+    def gather_relay(it, zc, yc):
         for d in reversed(outward(nz)):
             zc[d].wait_recv()
-            got = ag.at[it, y, (z + nz - d) % nz]
+            zz = (z + nz - d) % nz
+            got = wire.at[it, y, zz]
             for e in outward(ny):
                 cp = rcopy(got, got, ydev(e))
                 cp.start()
-                yc.append(cp)
-        for cp in yc:
-            cp.wait()
+                yc.append((cp, e, zz))
+
+    def gather_end(it, zc, yc):
+        def use(yy, zz):
+            v = unpack(wire.at[0, yy, zz])
+            if it:
+                v = v - acol[...] * unpack(wire.at[1, yy, zz])
+            ag[yy, zz] = v.astype(BF16)
+
+        for zz in range(nz):
+            use(y, zz)
+        for cp, e, zz in yc:
+            cp.wait_recv()
+            use((y + ny - e) % ny, zz)
+        for cp, e, zz in yc:
+            cp.wait_send()
         for d in zc:
             zc[d].wait_send()
 
-    def adjoint(it):
+    def adjoint():
         def slot(k, carry):
             r = tab[0, k]
-            p = jnp.dot(ag[it, r // nz, r % nz], green[k], preferred_element_type=F32)
+            p = jnp.dot(ag[r // nz, r % nz], green[k], preferred_element_type=F32)
             sums[k] = p + sums[tab[2, k]]
             return carry
 
-        lax.fori_loop(0, slots, slot, 0, unroll=4)
+        lax.fori_loop(0, slots, slot, 0, unroll=16)
 
     def forward(it):
         def slot(k, carry):
@@ -129,7 +150,7 @@
             sums[k] = p + sums[tab[3, k]]
             return carry
 
-        lax.fori_loop(0, slots, slot, 0, unroll=4)
+        lax.fori_loop(0, slots, slot, 0, unroll=16)
 
     def scatter_tm(it):
         order = outward(nx) + [0]
@@ -219,44 +240,55 @@
             v = v + unpack(z_recv.at[it, d - 1])
         return wcol[...] * v
 
-    def all_reduce(n, v):
-        for ref, me, count, dev in (
-            (ar_z, z, nz, zdev), (ar_p, y * nx + x, ny * nx, pdev), (ar_c, c, nc, None),
-        ):
-            ref[n, me] = v
-            copies = [
-                rcopy(ref.at[n, me], ref.at[n, me], dev(d) if dev else cdev())
-                for d in range(count - 1, 0, -1)
-            ]
-            for cp in copies:
-                cp.start()
-            for cp in copies:
-                cp.wait()
-            v = ref[n, 0]
-            for j in range(1, count):
-                v = v + ref[n, j]
+    stages = ((ar_z, z, nz, zdev), (ar_p, y * nx + x, ny * nx, pdev), (ar_c, c, nc, None))
+
+    def reduce_begin(n, stage, v):
+        ref, me, count, dev = stages[stage]
+        ref[n, me] = v
+        copies = [
+            rcopy(ref.at[n, me], ref.at[n, me], dev(d) if dev else cdev())
+            for d in range(count - 1, 0, -1)
+        ]
+        for cp in copies:
+            cp.start()
+        return copies
+
+    def reduce_end(n, stage, copies):
+        ref, me, count, dev = stages[stage]
+        for cp in copies:
+            cp.wait()
+        v = ref[n, 0]
+        for j in range(1, count):
+            v = v + ref[n, j]
         return v
 
     def rowsum(a):
         return jnp.sum(a, axis=0, keepdims=True)
 
-    gather_src(0)
-    load.wait()
-    adjoint(0)
+    hops = gather_begin(0, wcol[...] * res_out[...])
+    gather_relay(0, *hops)
+    gather_end(0, *hops)
+    loads[3].wait()
+    adjoint()
     gamma0 = scatter_tm(0)
     gather_tm(0)
     forward(0)
     image0 = scatter_src(0)
     norms = jnp.concatenate([gamma0, rowsum(image0 * image0), jnp.zeros((6, BS), F32)], axis=0)
-    norms = all_reduce(0, norms)
+    copies = reduce_begin(0, 0, norms)
+    own[per] = image0
+    hops = gather_begin(1, wcol[...] * image0)
+    copies = reduce_begin(0, 1, reduce_end(0, 0, copies))
+    gather_relay(1, *hops)
+    copies = reduce_begin(0, 2, reduce_end(0, 1, copies))
+    norms = reduce_end(0, 2, copies)
     gamma0 = norms[0:1]
     norm0 = norms[1:2]
     alpha0 = gamma0 / (norm0 + EPSILON)
-    own[per] = image0
-    residual = res_out[...] - alpha0 * image0
-    res_out[...] = residual
-    gather_src(1)
-    adjoint(1)
+    acol[...] = jnp.transpose(jnp.broadcast_to(alpha0, (BS, BS)))
+    gather_end(1, *hops)
+    res_out[...] = res_out[...] - alpha0 * own[per]
+    adjoint()
     gamma1 = scatter_tm(1)
     gather_tm(1)
     forward(1)
@@ -270,7 +302,8 @@
         ],
         axis=0,
     )
-    norms = all_reduce(1, norms)
+    for stage in range(3):
+        norms = reduce_end(1, stage, reduce_begin(1, stage, norms))
     gamma1 = norms[0:1]
     beta = gamma1 / (gamma0 + EPSILON)
     norm1 = norms[1:2] + beta * (2.0 * norms[2:3] + beta * norm0)
@@ -313,6 +346,7 @@
     tm_copies = nx + (nx - 1) + (nx - 1) + nx
     copies = 2 * (2 * src_copies + tm_copies + (NZ - 1) + (ny * nx - 1) + (NC - 1))
     vmem = pl.BlockSpec(memory_space=pltpu.VMEM)
+    hbm = pl.BlockSpec(memory_space=pltpu.HBM)
     tile = (BS, BS)
     coded = (BS + 16, BS)
     sol, res, mis = pl.pallas_call(
@@ -324,13 +358,17 @@
         ),
         in_specs=[
             pl.BlockSpec(memory_space=pltpu.SMEM),
-            pl.BlockSpec(memory_space=pl.ANY),
-            vmem, vmem, vmem,
+            hbm, hbm, hbm, hbm,
         ],
         out_specs=(vmem, vmem, vmem),
         scratch_shapes=[
             pltpu.VMEM((slots,) + tile, BF16),
-            pltpu.VMEM((2, ny, NZ) + tile, BF16),
+            pltpu.VMEM(tile, F32),
+            pltpu.VMEM((1, BS), F32),
+            pltpu.VMEM((cb, BS), F32),
+            pltpu.VMEM((ny, NZ) + tile, BF16),
+            pltpu.VMEM((2, ny, NZ) + coded, jnp.int16),
+            pltpu.VMEM(tile, F32),
             pltpu.VMEM((slots + 1,) + tile, F32),
             pltpu.VMEM((2, nx * per) + tile, F32),
             pltpu.VMEM((2, nx * per) + tile, F32),
@@ -350,7 +388,7 @@
             pltpu.VMEM((2, NC, 8, BS), F32),
             pltpu.SemaphoreType.DMA((copies,)),
             pltpu.SemaphoreType.DMA((copies,)),
-            pltpu.SemaphoreType.DMA,
+            pltpu.SemaphoreType.DMA((4,)),
         ],
         compiler_params=pltpu.CompilerParams(
             collective_id=0, has_side_effects=True, vmem_limit_bytes=48 * 1024 * 1024

time: 184 us -> 162 us (0.88)
  Pallas kernels: 174 us -> 153 us
    pallas_call x1, Pallas kernels: 174 us -> 153 us  [shards(): pl.pallas_call(functools.partial(kernel, ny, nx, float(src * tm * BS), sl...]
where the time goes in v2:
time: 162 us
  Pallas kernels  153 us (94%)
  local copies, waits for them, and re-layouts  7.05 us (4%)
    pallas_call x1, Pallas kernels, shards(): pl.pallas_call(functools.partial(kernel, ny, nx, float(src * tm * BS), sl...  153 us
    unnamed x11, local copies, waits for them, and re-layouts  6.29 us

profile of v2, /device:TPU:1, one launch (start us, length us, event | category | flops | bytes accessed | tf_op | source)
XLA Modules:
  0.0 162.2 jit_solution(11099397749704878874)
XLA Ops:
  0.6 0.7 compare_bitcast_fusion
  1.3 0.9 select_reduce_fusion
  2.2 0.8 stack.19
  3.0 0.0 copy-start
  3.0 2.2 %copy-done = bf16[1,128,128,128]{3,2,1,0:T(8,128)(2,1)S(1)} copy-done((bf16[1,128,128,128]{3,2,1,0:T(8,128)(2,1)S(1)}, bf16[1,128,128,128]{3,2,1,0:T(8,128)(2,1)}, u32[]{:S(2)}) %copy-start) | copy-done | bytes 4194328
  5.2 0.0 copy-start.1
  5.2 0.8 copy-done.1
  6.0 0.0 copy-start.2
  6.0 0.7 copy-done.2
  6.8 0.0 copy-start.3
  6.8 0.7 copy-done.3
  7.4 152.9 %shard_map.94 = (f32[512,128]{1,0:T(8,128)S(1)}, f32[128,128]{1,0:T(8,128)S(1)}, f32[2,128]{1,0:T(2,128)S(1)}) custom-call(s32[8,128]{1,0:T(8,128)S(1)} %compare_select_fusion.tab, bf16[128,128,128]{2,1,0:T(8,128)(2,1)S(1)} %bitcast.12, f32[128,128]{1,0:T(8,128)S(1)} %bitcast.14, f32[1,128]{1,0:T(1,128)S(1)} %copy-done.3, f32[32,128]{1,0:T(8,128)S(1)} %bitcast.15), custom_call_target="tpu_custom_call" | custom-call | tf_op jit(solution)/shard_map/pallas_call | solution.py:352
  160.3 0.7 copy.13
  161.0 0.6 copy.14
  161.6 0.6 copy.15
  (1 shorter events, 0.0 us)
Async XLA Ops:
  3.0 2.2 %copy-start = (bf16[1,128,128,128]{3,2,1,0:T(8,128)(2,1)S(1)}, bf16[1,128,128,128]{3,2,1,0:T(8,128)(2,1)}, u32[]{:S(2)}) copy-start(bf16[1,128,128,128]{3,2,1,0:T(8,128)(2,1)} %param.7) | copy-start | bytes 12582916
  5.2 0.8 copy-start.1
  6.0 0.7 copy-start.2
  6.8 0.7 copy-start.3

commit v3 on v2

--- a/solution.py
+++ b/solution.py
@@ -38,9 +38,9 @@
 
 def kernel(
     ny, nx, total_rows, slots, cb,
-    tab, green_hbm, data_hbm, weight_hbm, gain_hbm,
+    rows, cols, live, green_hbm, data_hbm, weight_hbm, gain_hbm,
     sol_out, res_out, mis_out,
-    green, data, weight, gain, ag, wire, acol, sums, core_send, core_recv, x_send, x_recv, tb, y_send, y_recv, z_send, z_recv,
+    tabv, tab, green, data, weight, gain, ag, wire, acol, sums, core_send, core_recv, x_send, x_recv, tb, y_send, y_recv, z_send, z_recv,
     wcol, gcol, steep, own, ar_z, ar_p, ar_c,
     ssem, rsem, lsem,
 ):
@@ -89,6 +89,7 @@
 
     for cp in loads[:3]:
         cp.wait()
+    tabv[...] = jnp.zeros((8, slots), jnp.int32)
     wcol[...] = jnp.transpose(jnp.broadcast_to(weight[...], (BS, BS)))
     for i in range(per):
         row = gain[pl.ds(t * per + i, 1), :]
@@ -102,7 +103,7 @@
         mine = wire.at[it, y, z]
         zc = {d: rcopy(mine, mine, zdev(d)) for d in outward(nz)}
         yc = [(rcopy(mine, mine, ydev(e)), e, z) for e in outward(ny)]
-        for d in outward(nz):
+        for d in reversed(outward(nz)):
             zc[d].start()
         for cp, e, zz in yc:
             cp.start()
@@ -135,6 +136,25 @@
         for d in zc:
             zc[d].wait_send()
 
+    def tables():
+        jj = lax.broadcasted_iota(jnp.int32, (slots, slots), 0)
+        kk = lax.broadcasted_iota(jnp.int32, (slots, slots), 1)
+
+        def latest(hit):
+            j = jnp.max(jnp.where(hit, jj, -1), axis=0, keepdims=True)
+            return jnp.where(j < 0, slots, j)
+
+        tabv[0:1, :] = rows[...]
+        tabv[1:2, :] = cols[...]
+        for n, key in enumerate((cols, rows)):
+            lived = jnp.where(live[...] != 0, key[...], -1)
+            down = jnp.transpose(jnp.broadcast_to(lived, (slots, slots)))
+            tabv[2 + n : 3 + n, :] = latest((down == key[...]) & (jj < kk))
+            tabv[4 + n : 5 + n, :] = latest(down == kk)
+        cp = pltpu.make_async_copy(tabv, tab, lsem.at[4])
+        cp.start()
+        cp.wait()
+
     def adjoint():
         def slot(k, carry):
             r = tab[0, k]
@@ -142,7 +162,7 @@
             sums[k] = p + sums[tab[2, k]]
             return carry
 
-        lax.fori_loop(0, slots, slot, 0, unroll=16)
+        lax.fori_loop(0, slots, slot, 0, unroll=32)
 
     def forward(it):
         def slot(k, carry):
@@ -150,68 +170,57 @@
             sums[k] = p + sums[tab[3, k]]
             return carry
 
-        lax.fori_loop(0, slots, slot, 0, unroll=16)
-
-    def scatter_tm(it):
-        order = outward(nx) + [0]
+        lax.fori_loop(0, slots, slot, 0, unroll=32)
+
+    def exchange_tm(it):
         cc = []
-        for d in order:
-            xx = (x + d) % nx
-            for i in range(per):
-                b = xx * nc * per + (1 - c) * per + i
-                core_send[it, xx * per + i] = sums[tab[4, b]]
-            part = pl.ds(xx * per, per)
-            cp = rcopy(core_send.at[it, part], core_recv.at[it, part], cdev())
+        for i in range(per):
+            for d in outward(nx) + [0]:
+                xx = (x + d) % nx
+                core_send[it, i, xx] = sums[tab[4, (xx * nc + 1 - c) * per + i]]
+            cp = rcopy(core_send.at[it, i], core_recv.at[it, i], cdev())
             cp.start()
             cc.append(cp)
-        xc = []
-        for j, d in enumerate(order):
-            xx = (x + d) % nx
-            cc[j].wait()
-            for i in range(per):
-                b = xx * nc * per + c * per + i
-                v = sums[tab[4, b]] + core_recv[it, xx * per + i]
+        xc = {}
+        for i in range(per):
+            cc[i].wait()
+            for d in outward(nx) + [0]:
+                xx = (x + d) % nx
+                v = sums[tab[4, (xx * nc + c) * per + i]] + core_recv[it, i, xx]
                 if d:
                     pack(x_send.at[it, d - 1, i], v)
+                    xc[i, d] = rcopy(x_send.at[it, d - 1, i], x_recv.at[it, d - 1, i], xdev(d))
+                    xc[i, d].start()
                 else:
                     own[i] = v
-            if d:
-                cp = rcopy(x_send.at[it, d - 1], x_recv.at[it, d - 1], xdev(d))
-                cp.start()
-                xc.append(cp)
-        for cp in xc:
-            cp.wait()
         gamma = jnp.zeros((1, BS), F32)
+        gc, fc = {}, []
         for i in range(per):
             v = own[i]
             for d in range(1, nx):
+                xc[i, d].wait()
                 v = v + unpack(x_recv.at[it, d - 1, i])
             st = gcol[i] * jnp.transpose(v)
             steep[it, i] = st
             gamma = gamma + jnp.sum(st * st, axis=0, keepdims=True)
+            mine = tb.at[it, t * per + i]
             tb[it, t * per + i] = (gcol[i] * st).astype(BF16)
-        return gamma
-
-    def gather_tm(it):
-        def part(xx, cc):
-            return tb.at[it, pl.ds((xx * nc + cc) * per, per)]
-
-        mine = part(x, c)
-        xc = {d: rcopy(mine, mine, xdev(d)) for d in outward(nx)}
-        for d in xc:
-            xc[d].start()
-        fc = [rcopy(mine, mine, cdev())]
-        fc[0].start()
-        for d in reversed(outward(nx)):
-            xc[d].wait_recv()
-            got = part((x + nx - d) % nx, c)
-            cp = rcopy(got, got, cdev())
-            cp.start()
-            fc.append(cp)
+            for d in outward(nx):
+                gc[i, d] = rcopy(mine, mine, xdev(d))
+                gc[i, d].start()
+            fc.append(rcopy(mine, mine, cdev()))
+            fc[-1].start()
+        for i in range(per):
+            for d in reversed(outward(nx)):
+                gc[i, d].wait_recv()
+                got = tb.at[it, (((x + nx - d) % nx) * nc + c) * per + i]
+                fc.append(rcopy(got, got, cdev()))
+                fc[-1].start()
         for cp in fc:
             cp.wait()
-        for d in xc:
-            xc[d].wait_send()
+        for key in gc:
+            gc[key].wait_send()
+        return gamma
 
     def scatter_src(it):
         order = outward(nz) + [0]
@@ -266,12 +275,12 @@
         return jnp.sum(a, axis=0, keepdims=True)
 
     hops = gather_begin(0, wcol[...] * res_out[...])
+    tables()
     gather_relay(0, *hops)
     gather_end(0, *hops)
     loads[3].wait()
     adjoint()
-    gamma0 = scatter_tm(0)
-    gather_tm(0)
+    gamma0 = exchange_tm(0)
     forward(0)
     image0 = scatter_src(0)
     norms = jnp.concatenate([gamma0, rowsum(image0 * image0), jnp.zeros((6, BS), F32)], axis=0)
@@ -289,8 +298,7 @@
     gather_end(1, *hops)
     res_out[...] = res_out[...] - alpha0 * own[per]
     adjoint()
-    gamma1 = scatter_tm(1)
-    gather_tm(1)
+    gamma1 = exchange_tm(1)
     forward(1)
     part1 = scatter_src(1)
     image0 = own[per]
@@ -317,33 +325,15 @@
         sol_out[pl.ds(i * BS, BS), :] = (alpha0 + alpha1 * beta) * steep[0, i] + alpha1 * steep[1, i]
 
 
-def tables(rows, cols, live, slots, rb, cb):
-    j = jnp.arange(slots, dtype=jnp.int32)
-    lived = live != 0
-    before = (j[None, :] < j[:, None]) & lived[None, :]
-
-    def prev(key):
-        return jnp.max(jnp.where(before & (key[None, :] == key[:, None]), j[None, :], -1), axis=1)
-
-    def last(key):
-        hit = lived[None, :] & (key[None, :] == j[:, None])
-        return jnp.max(jnp.where(hit, j[None, :], -1), axis=1)
-
-    out = jnp.stack([rows, cols, prev(cols), prev(rows), last(cols), last(rows), rows, cols])
-    return jnp.where(out < 0, slots, out)
-
-
 def shards(green, block_rows, block_cols, block_live, data, row_weight, source_gain):
     slots = green.shape[1]
     src, tm = lax.axis_size("src"), lax.axis_size("tm")
     ny, nx = src // NZ, tm // NC
     cb = source_gain.shape[0] // BS
-    rb = src
     per = cb // tm
     datasets = data.shape[2]
-    tab = tables(block_rows[0], block_cols[0], block_live[0], slots, rb, cb)
     src_copies = (NZ - 1) + (ny - 1) * NZ
-    tm_copies = nx + (nx - 1) + (nx - 1) + nx
+    tm_copies = per * (1 + (nx - 1) + (nx - 1) + nx)
     copies = 2 * (2 * src_copies + tm_copies + (NZ - 1) + (ny * nx - 1) + (NC - 1))
     vmem = pl.BlockSpec(memory_space=pltpu.VMEM)
     hbm = pl.BlockSpec(memory_space=pltpu.HBM)
@@ -357,11 +347,12 @@
             jax.ShapeDtypeStruct((2, datasets), F32),
         ),
         in_specs=[
-            pl.BlockSpec(memory_space=pltpu.SMEM),
-            hbm, hbm, hbm, hbm,
+            vmem, vmem, vmem, hbm, hbm, hbm, hbm,
         ],
         out_specs=(vmem, vmem, vmem),
         scratch_shapes=[
+            pltpu.VMEM((8, slots), jnp.int32),
+            pltpu.SMEM((8, slots), jnp.int32),
             pltpu.VMEM((slots,) + tile, BF16),
             pltpu.VMEM(tile, F32),
             pltpu.VMEM((1, BS), F32),
@@ -370,8 +361,8 @@
             pltpu.VMEM((2, ny, NZ) + coded, jnp.int16),
             pltpu.VMEM(tile, F32),
             pltpu.VMEM((slots + 1,) + tile, F32),
-            pltpu.VMEM((2, nx * per) + tile, F32),
-            pltpu.VMEM((2, nx * per) + tile, F32),
+            pltpu.VMEM((2, per, nx) + tile, F32),
+            pltpu.VMEM((2, per, nx) + tile, F32),
             pltpu.VMEM((2, nx - 1, per) + coded, jnp.int16),
             pltpu.VMEM((2, nx - 1, per) + coded, jnp.int16),
             pltpu.VMEM((2, cb) + tile, BF16),
@@ -388,12 +379,12 @@
             pltpu.VMEM((2, NC, 8, BS), F32),
             pltpu.SemaphoreType.DMA((copies,)),
             pltpu.SemaphoreType.DMA((copies,)),
-            pltpu.SemaphoreType.DMA((4,)),
+            pltpu.SemaphoreType.DMA((5,)),
         ],
         compiler_params=pltpu.CompilerParams(
             collective_id=0, has_side_effects=True, vmem_limit_bytes=48 * 1024 * 1024
         ),
-    )(tab, green[0], data[0], row_weight, source_gain.reshape(cb, BS))
+    )(block_rows, block_cols, block_live, green[0], data[0], row_weight, source_gain.reshape(cb, BS))
     return sol, res[None], mis
 
 

time: 162 us -> 145 us (0.90)
  Pallas kernels: 153 us -> 136 us
    pallas_call x1, Pallas kernels: 153 us -> 136 us  [shards(): pl.pallas_call(functools.partial(kernel, ny, nx, float(src * tm * BS), sl...]
    unnamed x11 -> x17, local copies, waits for them, and re-layouts: 6.29 us -> 8.25 us
where the time goes in v3:
time: 145 us
  Pallas kernels  136 us (94%)
  local copies, waits for them, and re-layouts  8.25 us (6%)
    pallas_call x1, Pallas kernels, shards(): pl.pallas_call(functools.partial(kernel, ny, nx, float(src * tm * BS), sl...  136 us
    unnamed x17, local copies, waits for them, and re-layouts  8.25 us

profile of v3, /device:TPU:1, one launch (start us, length us, event | category | flops | bytes accessed | tf_op | source)
XLA Modules:
  0.0 145.0 jit_solution(5413518019429487260)
XLA Ops:
  0.6 0.0 copy-start
  0.6 2.2 %copy-done = bf16[1,128,128,128]{3,2,1,0:T(8,128)(2,1)S(1)} copy-done((bf16[1,128,128,128]{3,2,1,0:T(8,128)(2,1)S(1)}, bf16[1,128,128,128]{3,2,1,0:T(8,128)(2,1)}, u32[]{:S(2)}) %copy-start) | copy-done | bytes 4194328
  2.8 0.0 copy-start.1
  2.8 0.8 copy-done.1
  3.7 0.0 copy-start.2
  3.7 0.7 copy-done.2
  4.4 0.0 copy-start.3
  4.4 0.7 copy-done.3
  5.0 0.0 copy-start.4
  5.0 0.7 copy-done.4
  5.7 0.0 copy-start.5
  5.7 0.7 copy-done.5
  6.3 0.0 copy-start.6
  6.3 0.7 copy-done.6
  7.0 136.1 %shard_map.94 = (f32[512,128]{1,0:T(8,128)S(1)}, f32[128,128]{1,0:T(8,128)S(1)}, f32[2,128]{1,0:T(2,128)S(1)}) custom-call(s32[1,128]{1,0:T(1,128)S(1)} %copy-done.3, s32[1,128]{1,0:T(1,128)S(1)} %copy-done.4, s32[1,128]{1,0:T(1,128)S(1)} %copy-done.5, bf16[128,128,128]{2,1,0:T(8,128)(2,1)S(1)} %bitcast.4, f32[128,128]{1,0:T(8,128)S(1)} %bitcast.5, ...), custom_call_target="tpu_custom_call" | custom-call | tf_op jit(solution)/shard_map/pallas_call | solution.py:342
  143.1 0.7 copy.13
  143.8 0.6 copy.14
  144.4 0.6 copy.15
Async XLA Ops:
  0.6 2.2 %copy-start = (bf16[1,128,128,128]{3,2,1,0:T(8,128)(2,1)S(1)}, bf16[1,128,128,128]{3,2,1,0:T(8,128)(2,1)}, u32[]{:S(2)}) copy-start(bf16[1,128,128,128]{3,2,1,0:T(8,128)(2,1)} %param.7) | copy-start | bytes 12582916
  2.8 0.8 copy-start.1
  3.7 0.7 copy-start.2
  4.4 0.7 copy-start.3
  5.0 0.7 copy-start.4
  5.7 0.7 copy-start.5
  6.3 0.7 copy-start.6

commit v4 on v3

--- a/solution.py
+++ b/solution.py
@@ -28,11 +28,11 @@
     e = jnp.ceil(jnp.log2(top))
     q = jnp.floor(v * (jnp.exp2(-e) * STEPS) + 0.5)
     ref[0:BS, :] = q.astype(jnp.int32).astype(jnp.int16)
-    ref[BS : BS + 16, :] = jnp.broadcast_to(e.astype(jnp.int32), (16, BS)).astype(jnp.int16)
+    ref[BS : BS + 8, :] = jnp.broadcast_to(e.astype(jnp.int32), (8, BS)).astype(jnp.int16)
 
 
 def unpack(ref):
-    e = ref[BS : BS + 16, :].astype(jnp.int32).astype(F32)[0:1]
+    e = ref[BS : BS + 8, :].astype(jnp.int32).astype(F32)[0:1]
     return ref[0:BS, :].astype(jnp.int32).astype(F32) * (jnp.exp2(e) * (1.0 / STEPS))
 
 
@@ -96,10 +96,10 @@
         gcol[i] = jnp.transpose(jnp.broadcast_to(row, (BS, BS)))
     sums[slots] = jnp.zeros((BS, BS), F32)
     res_out[...] = wcol[...] * data[...]
+    pack(wire.at[0, y, z], jnp.transpose(wcol[...] * res_out[...]))
     pl.semaphore_wait(barrier, len(peers))
 
-    def gather_begin(it, v):
-        pack(wire.at[it, y, z], jnp.transpose(v))
+    def gather_begin(it):
         mine = wire.at[it, y, z]
         zc = {d: rcopy(mine, mine, zdev(d)) for d in outward(nz)}
         yc = [(rcopy(mine, mine, ydev(e)), e, z) for e in outward(ny)]
@@ -274,7 +274,7 @@
     def rowsum(a):
         return jnp.sum(a, axis=0, keepdims=True)
 
-    hops = gather_begin(0, wcol[...] * res_out[...])
+    hops = gather_begin(0)
     tables()
     gather_relay(0, *hops)
     gather_end(0, *hops)
@@ -286,7 +286,8 @@
     norms = jnp.concatenate([gamma0, rowsum(image0 * image0), jnp.zeros((6, BS), F32)], axis=0)
     copies = reduce_begin(0, 0, norms)
     own[per] = image0
-    hops = gather_begin(1, wcol[...] * image0)
+    pack(wire.at[1, y, z], jnp.transpose(wcol[...] * image0))
+    hops = gather_begin(1)
     copies = reduce_begin(0, 1, reduce_end(0, 0, copies))
     gather_relay(1, *hops)
     copies = reduce_begin(0, 2, reduce_end(0, 1, copies))
@@ -338,7 +339,7 @@
     vmem = pl.BlockSpec(memory_space=pltpu.VMEM)
     hbm = pl.BlockSpec(memory_space=pltpu.HBM)
     tile = (BS, BS)
-    coded = (BS + 16, BS)
+    coded = (BS + 8, BS)
     sol, res, mis = pl.pallas_call(
         functools.partial(kernel, ny, nx, float(src * tm * BS), slots, cb),
         out_shape=(
@@ -358,18 +359,18 @@
             pltpu.VMEM((1, BS), F32),
             pltpu.VMEM((cb, BS), F32),
             pltpu.VMEM((ny, NZ) + tile, BF16),
-            pltpu.VMEM((2, ny, NZ) + coded, jnp.int16),
+            pltpu.VMEM((3, ny, NZ) + coded, jnp.int16),
             pltpu.VMEM(tile, F32),
             pltpu.VMEM((slots + 1,) + tile, F32),
             pltpu.VMEM((2, per, nx) + tile, F32),
             pltpu.VMEM((2, per, nx) + tile, F32),
-            pltpu.VMEM((2, nx - 1, per) + coded, jnp.int16),
-            pltpu.VMEM((2, nx - 1, per) + coded, jnp.int16),
+            pltpu.VMEM((3, nx - 1, per) + coded, jnp.int16),
+            pltpu.VMEM((3, nx - 1, per) + coded, jnp.int16),
             pltpu.VMEM((2, cb) + tile, BF16),
-            pltpu.VMEM((2, ny - 1, NZ) + coded, jnp.int16),
-            pltpu.VMEM((2, ny - 1, NZ) + coded, jnp.int16),
-            pltpu.VMEM((2, NZ - 1) + coded, jnp.int16),
-            pltpu.VMEM((2, NZ - 1) + coded, jnp.int16),
+            pltpu.VMEM((3, ny - 1, NZ) + coded, jnp.int16),
+            pltpu.VMEM((3, ny - 1, NZ) + coded, jnp.int16),
+            pltpu.VMEM((3, NZ - 1) + coded, jnp.int16),
+            pltpu.VMEM((3, NZ - 1) + coded, jnp.int16),
             pltpu.VMEM(tile, F32),
             pltpu.VMEM((per,) + tile, F32),
             pltpu.VMEM((2, per) + tile, F32),

time: 145 us -> 142 us (0.979)
  Pallas kernels: 136 us -> 133 us
    pallas_call x1, Pallas kernels: 136 us -> 133 us  [shards(): pl.pallas_call(functools.partial(kernel, ny, nx, float(src * tm * BS), sl...]
where the time goes in v4:
time: 142 us; the launch traced here: 141 us
  Pallas kernels  133 us (94%)
  local copies, waits for them, and re-layouts  8.25 us (6%)
    pallas_call x1, Pallas kernels, shards(): pl.pallas_call(functools.partial(kernel, ny, nx, float(src * tm * BS), sl...  133 us
    unnamed x17, local copies, waits for them, and re-layouts  8.25 us

profile of v4, /device:TPU:1, one launch (start us, length us, event | category | flops | bytes accessed | tf_op | source)
XLA Modules:
  0.0 141.4 jit_solution(16131132718838840448)
XLA Ops:
  0.6 0.0 copy-start
  0.6 2.2 %copy-done = bf16[1,128,128,128]{3,2,1,0:T(8,128)(2,1)S(1)} copy-done((bf16[1,128,128,128]{3,2,1,0:T(8,128)(2,1)S(1)}, bf16[1,128,128,128]{3,2,1,0:T(8,128)(2,1)}, u32[]{:S(2)}) %copy-start) | copy-done | bytes 4194328
  2.8 0.0 copy-start.1
  2.8 0.8 copy-done.1
  3.7 0.0 copy-start.2
  3.7 0.7 copy-done.2
  4.4 0.0 copy-start.3
  4.4 0.7 copy-done.3
  5.0 0.0 copy-start.4
  5.0 0.7 copy-done.4
  5.7 0.0 copy-start.5
  5.7 0.7 copy-done.5
  6.3 0.0 copy-start.6
  6.3 0.7 copy-done.6
  7.0 132.5 %shard_map.94 = (f32[512,128]{1,0:T(8,128)S(1)}, f32[128,128]{1,0:T(8,128)S(1)}, f32[2,128]{1,0:T(2,128)S(1)}) custom-call(s32[1,128]{1,0:T(1,128)S(1)} %copy-done.3, s32[1,128]{1,0:T(1,128)S(1)} %copy-done.4, s32[1,128]{1,0:T(1,128)S(1)} %copy-done.5, bf16[128,128,128]{2,1,0:T(8,128)(2,1)S(1)} %bitcast.4, f32[128,128]{1,0:T(8,128)S(1)} %bitcast.5, ...), custom_call_target="tpu_custom_call" | custom-call | tf_op jit(solution)/shard_map/pallas_call | solution.py:343
  139.5 0.7 copy.13
  140.2 0.6 copy.14
  140.9 0.6 copy.15
Async XLA Ops:
  0.6 2.2 %copy-start = (bf16[1,128,128,128]{3,2,1,0:T(8,128)(2,1)S(1)}, bf16[1,128,128,128]{3,2,1,0:T(8,128)(2,1)}, u32[]{:S(2)}) copy-start(bf16[1,128,128,128]{3,2,1,0:T(8,128)(2,1)} %param.7) | copy-start | bytes 12582916
  2.8 0.8 copy-start.1
  3.7 0.7 copy-start.2
  4.4 0.7 copy-start.3
  5.0 0.7 copy-start.4
  5.7 0.7 copy-start.5
  6.3 0.7 copy-start.6
